TPU v7x, 32 devices: a whole 2x2x4 slice. The times are simulated.
32 devices in a mesh: outer: 4 (over y, x), inner: 8 (over z, core).
Axes of the slice: x: 2, y: 2, z: 4, core: 2. Of those that a mesh axis runs over, the one named last changes fastest.
Arguments:
- queries: bfloat16 [8192, 1024], P(('outer', 'inner')), may hold values from -6 to 6
- keys: bfloat16 [2, 8192, 1024], P(None, ('outer', 'inner')), may hold values from -6 to 6
- values: bfloat16 [2, 8192, 1024], P(None, ('outer', 'inner')), may hold values from -6 to 6
- betas: float32 [2, 8, 8192], P(None, None, ('outer', 'inner')), may hold values from 0 to 2
- log_decay: float32 [8, 8192], P(None, ('outer', 'inner')), may hold values from -1 to 0
- out_gain: float32 [128], replicated, may hold values from 0.5 to 1.5
Outputs:
- mixed: bfloat16 [8192, 1024], P(('outer', 'inner'))
All inputs are finite; a program needn't handle non-finite values.
Results may differ from a plain program's by a relative error of at most 0.0018.
Values sent between devices are 32-bit elements; how exact they have to be, the bound alone decides.
A program may use at most 128 MiB of HBM per device.

v0:
```python
import functools

import jax
import jax.numpy as jnp
from jax import lax
from jax.experimental import pallas as pl
from jax.experimental.pallas import tpu as pltpu
from jax.sharding import PartitionSpec as P

BLOCK_LEN = 64
F32 = jnp.float32
BF16 = jnp.bfloat16


def split(x):
    high = x.astype(BF16)
    low = (x - high.astype(F32)).astype(BF16)
    return high, low


def dot(a, b):
    return lax.dot_general(a, b, (((1,), (0,)), ((), ())), preferred_element_type=F32)


def dot_t(a, b):
    return lax.dot_general(a, b, (((1,), (1,)), ((), ())), preferred_element_type=F32)


def wide(x):
    return jnp.concatenate(split(x), 1)


def mul(a, b):
    a2 = wide(a)
    bh, bl = split(b)
    if b.shape[1] == 128:
        row = jnp.concatenate([bh, bl], 1)
        both = dot(a2, jnp.concatenate([row, row], 0))
        return both[:, :128] + both[:, 128:]
    return dot(a2, jnp.concatenate([bh, bh], 0)) + dot(a2[:, :128], bl)


def mul_left(a, b):
    return dot(wide(a), jnp.concatenate([b, b], 0))


def add_right(x, y):
    return jnp.concatenate([x[:, :128], x[:, 128:] + y], 1)


def masks():
    span = BLOCK_LEN
    size = 2 * span
    row = lax.broadcasted_iota(jnp.int32, (size, size), 0)
    col = lax.broadcasted_iota(jnp.int32, (size, size), 1)
    row_t, col_t = row & (span - 1), col & (span - 1)
    row_rank = 2 * row_t + (row >= span).astype(jnp.int32)
    col_rank = 2 * col_t + (col >= span).astype(jnp.int32)
    differ = row_rank ^ col_rank
    eye = row == col
    eye_f = eye.astype(F32)
    lower = row_rank > col_rank
    c_mask = (col_t <= row_t) & (col < span)
    r_mask = (row_t <= col_t) & (row < span)
    levels = []
    width = 1
    while width < size:
        levels.append(
            (differ >= width) & (differ < 2 * width) & lower
        )
        width *= 2

    return row, col_t, row_t, eye, eye_f, lower, c_mask, r_mask, levels


def head_maps(blocks, heads_in, load, emit):
    span = BLOCK_LEN
    row, col_t, row_t, eye, eye_f, lower, c_mask, r_mask, levels = masks()
    work = []
    for i, n in [(i, n) for i in range(heads_in) for n in range(blocks)]:
        q_b, k_b, v_b, d_row, beta_row = load(i, n)
        d_col = jnp.sum(jnp.where(eye, d_row, 0.0), 1, keepdims=True)
        beta_col = jnp.sum(jnp.where(eye, beta_row, 0.0), 1, keepdims=True)
        c_col = jnp.sum(jnp.where(c_mask, d_row, 0.0), 1, keepdims=True)
        c_row = jnp.sum(jnp.where(r_mask, d_col, 0.0), 0, keepdims=True)
        gram = dot_t(k_b, k_b)
        k_f = k_b.astype(F32)
        q_f = q_b.astype(F32)
        ki_col = lax.rsqrt(jnp.sum(k_f * k_f, 1, keepdims=True) + 1e-06)
        ki_row = lax.rsqrt(jnp.sum(jnp.where(eye, gram, 0.0), 0, keepdims=True) + 1e-06)
        qi_col = lax.rsqrt(jnp.sum(q_f * q_f, 1, keepdims=True) + 1e-06)
        fall = jnp.exp(jnp.minimum(c_col - c_row, 0.0))
        low = jnp.where(lower, gram * (beta_col * ki_col) * ki_row * fall, 0.0)
        reach = dot_t(q_b, k_b) * qi_col * ki_row * fall[:span]
        reach = jnp.where(col_t[:span] <= row_t[:span], reach, 0.0)
        query = q_f * (qi_col * jnp.exp(c_col[:span]))
        work.append((k_b, v_b, beta_row, c_row, c_col, ki_row, ki_col, low, reach, query))

    inverse = [eye_f - jnp.where(levels[0], w[7], 0.0) for w in work]
    for mask in levels[1:]:
        part = [mul(jnp.where(mask, w[7], 0.0), t) for w, t in zip(work, inverse)]
        inverse = [t - mul(t, p) for t, p in zip(inverse, part)]

    states = [None] * heads_in
    for n in range(blocks):
        for i in range(heads_in):
            state = states[i]
            k_b, v_b, beta_row, c_row, c_col, ki_row, ki_col, low, reach, query = work[i * blocks + n]
            t = inverse[i * blocks + n] * beta_row
            written = jnp.concatenate(
                [mul_left(t * (ki_row * jnp.exp(c_row)), k_b), mul_left(t, v_b)], 1
            )
            got = mul(reach, written)
            reduced, local_out = query - got[:, :128], got[:, 128:]
            last = c_col[span - 1 : span, :]
            tail = jnp.exp(last - c_col) * ki_col
            wh, wl = split(written * tail)
            k_t = jnp.transpose(k_b.astype(F32)).astype(BF16)
            made = dot(jnp.concatenate([k_t, k_t], 1), jnp.concatenate([wh, wl], 0))
            trans = jnp.exp(last) * eye_f - made[:, :128]
            inject = made[:, 128:]
            if state is None:
                emit(i, n, reduced, local_out)
                states[i] = jnp.concatenate([trans, inject], 1)
            else:
                read = mul(reduced, state)
                emit(i, n, read[:, :128], read[:, 128:] + local_out)
                states[i] = add_right(mul(trans, state), inject)
    return states


def local_kernel(blocks, q_ref, k_ref, v_ref, s_ref, x_ref, c_ref, b_ref):
    def load(i, n):
        at = pl.ds(n * BLOCK_LEN, BLOCK_LEN)
        k_b = jnp.concatenate([k_ref[0, at, :], k_ref[1, at, :]], 0)
        v_b = jnp.concatenate([v_ref[0, at, :], v_ref[1, at, :]], 0)
        return q_ref[at, :], k_b, v_b, s_ref[0, n : n + 1, :], s_ref[0, blocks + n : blocks + n + 1, :]

    def emit(i, n, carried, base):
        at = pl.ds(n * BLOCK_LEN, BLOCK_LEN)
        c_ref[0, at, :] = carried
        b_ref[0, at, :] = base

    x_ref[0] = head_maps(blocks, 1, load, emit)[0]


def small_rows(betas, log_decay):
    heads, length = log_decay.shape
    blocks = length // BLOCK_LEN
    beta = betas.reshape(2, heads, blocks, BLOCK_LEN).transpose(1, 2, 0, 3)
    beta = beta.reshape(heads, blocks, 2 * BLOCK_LEN)
    decay = log_decay.reshape(heads, blocks, 1, BLOCK_LEN)
    decay = jnp.concatenate([decay, decay], 2).reshape(heads, blocks, 2 * BLOCK_LEN)
    small = jnp.concatenate([decay, beta], 1)
    return small


def local_phase(queries, keys, values, betas, log_decay):
    length = queries.shape[0]
    heads = betas.shape[1]
    blocks = length // BLOCK_LEN
    small = small_rows(betas, log_decay)
    return pl.pallas_call(
        functools.partial(local_kernel, blocks),
        grid=(heads,),
        in_specs=[
            pl.BlockSpec((length, 128), lambda h: (0, h)),
            pl.BlockSpec((2, length, 128), lambda h: (0, 0, h)),
            pl.BlockSpec((2, length, 128), lambda h: (0, 0, h)),
            pl.BlockSpec((1, 2 * blocks, 128), lambda h: (h, 0, 0)),
        ],
        out_specs=[
            pl.BlockSpec((1, 128, 256), lambda h: (h, 0, 0)),
            pl.BlockSpec((1, length, 128), lambda h: (h, 0, 0)),
            pl.BlockSpec((1, length, 128), lambda h: (h, 0, 0)),
        ],
        out_shape=[
            jax.ShapeDtypeStruct((heads, 128, 256), F32),
            jax.ShapeDtypeStruct((heads, length, 128), F32),
            jax.ShapeDtypeStruct((heads, length, 128), F32),
        ],
        name="local_phase",
    )(queries, keys, values, small)


def then(earlier, later):
    return add_right(mul(later[:, :128], earlier), later[:, 128:])


def normed(carried, base, state, gain):
    readout = mul(carried, state) + base
    mean_sq = jnp.mean(readout * readout, 1, keepdims=True)
    return (readout * lax.rsqrt(mean_sq + 1e-05) * gain).astype(BF16)


def whole_kernel(
    inner, outer, q_ref, k_ref, v_ref, s_ref, g_ref, o_ref,
    away, near, own, even_map, sent, got, groups, mine, ready, came, aside, beside, c_buf, b_buf,
    send0, recv0, send1, recv1, send2, recv2, send3, recv3, send4, recv4,
):
    mesh_id = pl.DeviceIdType.MESH
    length = q_ref.shape[0]
    blocks = length // BLOCK_LEN
    me = lax.axis_index("inner")
    group = lax.axis_index("outer")
    core, chip, chips = me % 2, me // 2, inner // 2
    partner = chip * 2 + 1 - core
    groups[...] = jnp.zeros_like(groups)
    barrier = pltpu.get_barrier_semaphore()
    for d in range(1, chips):
        pl.semaphore_signal(
            barrier, inc=1, device_id=(group, (chip + d) % chips * 2 + core), device_id_type=mesh_id
        )
    pl.semaphore_signal(barrier, inc=1, device_id=(group, partner), device_id_type=mesh_id)
    for d in range(1, outer):
        pl.semaphore_signal(barrier, inc=1, device_id=((group + d) % outer, me), device_id_type=mesh_id)
    pl.semaphore_wait(barrier, chips + outer - 1)

    def near_copy(turn):
        return pltpu.make_async_remote_copy(
            src_ref=away.at[turn], dst_ref=near.at[turn],
            send_sem=send0.at[turn], recv_sem=recv0.at[turn],
            device_id=(group, partner), device_id_type=mesh_id,
        )

    def map_copy(d):
        return pltpu.make_async_remote_copy(
            src_ref=sent.at[d], dst_ref=got.at[d],
            send_sem=send1.at[d], recv_sem=recv1.at[d],
            device_id=(group, (chip + d) % chips * 2 + core), device_id_type=mesh_id,
        )

    def chip_map(turn):
        near_copy(turn).wait()
        here, there = own[turn], near[turn]
        even = jnp.where(core == 0, here, there)
        odd = jnp.where(core == 0, there, here)
        even_map[turn] = even
        return then(even, odd)

    def step(turn, carry):
        far = (chip + turn + 1) % chips * 2
        heads = [far + core, far + 1 - core]

        def load(i, n):
            at = pl.ds(n * BLOCK_LEN, BLOCK_LEN)
            lanes = pl.ds(pl.multiple_of(heads[i] * 128, 128), 128)
            k_b = jnp.concatenate([k_ref[0, at, lanes], k_ref[1, at, lanes]], 0)
            v_b = jnp.concatenate([v_ref[0, at, lanes], v_ref[1, at, lanes]], 0)
            rows = s_ref[heads[i]]
            return q_ref[at, lanes], k_b, v_b, rows[n : n + 1], rows[blocks + n : blocks + n + 1]

        def emit(i, n, carried, base):
            at = pl.ds(n * BLOCK_LEN, BLOCK_LEN)
            c_buf[heads[i], at, :] = carried
            b_buf[heads[i], at, :] = base

        states = head_maps(blocks, 2, load, emit)
        away[turn] = states[1]
        near_copy(turn).start()
        own[turn] = states[0]

        @pl.when(turn > 0)
        def _():
            sent[turn] = chip_map(turn - 1)
            map_copy(turn).start()

        return carry

    lax.fori_loop(0, chips, step, 0)
    got[0] = chip_map(chips - 1)
    for d in range(1, chips):
        map_copy(d).wait()

    maps = [got[(chip - i + chips) % chips] for i in range(chips)]

    def tree(parts):
        if len(parts) == 1:
            return parts
        half = len(parts) // 2
        pairs = [then(parts[2 * i], parts[2 * i + 1]) for i in range(half)]
        return pairs

    level = maps
    levels = [maps]
    while len(level) > 1:
        level = tree(level)
        levels.append(level)
    mine[...] = level[0]

    def group_copy(d):
        return pltpu.make_async_remote_copy(
            src_ref=mine, dst_ref=groups.at[d],
            send_sem=send2.at[d], recv_sem=recv2.at[d],
            device_id=((group + d) % outer, me), device_id_type=mesh_id,
        )

    for d in range(1, outer):

        @pl.when(group + d < outer)
        def _():
            group_copy(d).start()

    before = {}
    for i in range(1, chips):
        low = i & -i
        height = low.bit_length() - 1
        part = levels[height][(i - low) >> height]
        before[i] = part if i == low else then(before[i - low], part)
    left = wide(jnp.concatenate([before[i][:, :128] for i in range(1, chips)], 0))
    right = jnp.concatenate([before[i][:, 128:] for i in range(1, chips)], 0)

    for d in range(1, outer):

        @pl.when(group + d < outer)
        def _():
            group_copy(d).wait_send()

        @pl.when(group - d >= 0)
        def _():
            group_copy(d).wait_recv()

    start = jnp.zeros((128, 128), F32)
    for g in range(outer - 1):
        pair = groups[(group - g + outer) % outer]
        moved = mul(pair[:, :128], start) + pair[:, 128:]
        start = jnp.where(g < group, moved, start)

    sh, sl = split(start)
    row = jnp.concatenate([sh, sl], 1)
    both = dot(left, jnp.concatenate([row, row], 0))
    ready[0] = start
    ready[pl.ds(1, chips - 1)] = (both[:, :128] + both[:, 128:] + right).reshape(chips - 1, 128, 128)

    def back_copy(d):
        to = (chip + d) % chips
        return pltpu.make_async_remote_copy(
            src_ref=ready.at[to], dst_ref=came.at[d],
            send_sem=send3.at[d], recv_sem=recv3.at[d],
            device_id=(group, to * 2 + core), device_id_type=mesh_id,
        )

    def side_copy(d):
        return pltpu.make_async_remote_copy(
            src_ref=aside.at[d], dst_ref=beside.at[d],
            send_sem=send4.at[d], recv_sem=recv4.at[d],
            device_id=(group, partner), device_id_type=mesh_id,
        )

    for d in range(1, chips):
        back_copy(d).start()

    def out(head, state):
        lanes = pl.ds(pl.multiple_of(head * 128, 128), 128)
        o_ref[:, lanes] = normed(c_buf[head], b_buf[head], state, g_ref[...])

    for d in range(chips):
        if d:
            back_copy(d).wait()
            enter = came[d]
        else:
            enter = ready[chip]
        pair = even_map[chips - 1 - d]
        after = mul(pair[:, :128], enter) + pair[:, 128:]
        aside[d] = jnp.where(core == 0, after, enter)
        side_copy(d).start()
        far = (chip - d + chips) % chips * 2
        out(far + core, jnp.where(core == 0, enter, after))
        if d:
            side_copy(d - 1).wait()
            out((chip - d + 1 + chips) % chips * 2 + 1 - core, beside[d - 1])
    side_copy(chips - 1).wait()
    out((chip + 1) % chips * 2 + 1 - core, beside[chips - 1])


def whole(inner, outer, queries, keys, values, betas, log_decay, out_gain):
    length, width = queries.shape
    vmem = pl.BlockSpec(memory_space=pltpu.VMEM)
    dma = pltpu.SemaphoreType.DMA
    return pl.pallas_call(
        functools.partial(whole_kernel, inner, outer),
        in_specs=[vmem] * 5,
        out_specs=vmem,
        out_shape=jax.ShapeDtypeStruct((length, width), BF16),
        scratch_shapes=[
            *[pltpu.VMEM((inner // 2, 128, 256), F32)] * 6,
            pltpu.VMEM((outer, 128, 256), F32),
            pltpu.VMEM((128, 256), F32),
            *[pltpu.VMEM((inner // 2, 128, 128), F32)] * 4,
            *[pltpu.VMEM((inner, length, 128), F32)] * 2,
            *[dma((inner // 2,))] * 4,
            *[dma((outer,))] * 2,
            *[dma((inner // 2,))] * 4,
        ],
        compiler_params=pltpu.CompilerParams(collective_id=0, has_side_effects=True),
        name="whole",
    )(queries, keys, values, small_rows(betas, log_decay), out_gain.reshape(1, 128))


HIGHEST = lax.Precision.HIGHEST


def join(earlier, later):
    moved = jnp.einsum("hde,hef->hdf", later[..., :128], earlier, precision=HIGHEST)
    return jnp.concatenate([moved[..., :128], moved[..., 128:] + later[..., 128:]], -1)


def entering(pairs, axis, begin):
    gathered = lax.all_gather(pairs, axis)

    def one(hop, state):
        return join(state, lax.dynamic_index_in_dim(gathered, hop, 0, False))

    return lax.fori_loop(0, lax.axis_index(axis), one, begin)


def exchange_plain(pairs):
    eye = jnp.concatenate([jnp.eye(128, dtype=F32), jnp.zeros((128, 128), F32)], 1)
    begin = jnp.zeros_like(pairs) + eye
    before = entering(pairs, "inner", begin)
    through = join(before, pairs)
    last = lax.axis_index("inner") == lax.axis_size("inner") - 1
    total = lax.psum(jnp.where(last, through, 0.0), "inner")
    start = entering(total, "outer", begin)
    return join(start, before)[..., 128:]


def finish_kernel(c_ref, b_ref, e_ref, g_ref, o_ref):
    readout = mul(c_ref[0], e_ref[0]) + b_ref[0]
    mean_sq = jnp.mean(readout * readout, 1, keepdims=True)
    o_ref[...] = (readout * lax.rsqrt(mean_sq + 1e-05) * g_ref[...]).astype(BF16)


def finish(carried, base, state, out_gain):
    heads, length, _ = carried.shape
    return pl.pallas_call(
        finish_kernel,
        grid=(heads,),
        in_specs=[
            pl.BlockSpec((1, length, 128), lambda h: (h, 0, 0)),
            pl.BlockSpec((1, length, 128), lambda h: (h, 0, 0)),
            pl.BlockSpec((1, 128, 128), lambda h: (h, 0, 0)),
            pl.BlockSpec((1, 128), lambda h: (0, 0)),
        ],
        out_specs=pl.BlockSpec((length, 128), lambda h: (0, h)),
        out_shape=jax.ShapeDtypeStruct((length, heads * 128), BF16),
        name="finish",
    )(carried, base, state, out_gain.reshape(1, 128))


def per_device(inner, outer, queries, keys, values, betas, log_decay, out_gain):
    heads = betas.shape[1]
    if inner == heads:
        return whole(inner, outer, queries, keys, values, betas, log_decay, out_gain)
    pairs, carried, base = local_phase(queries, keys, values, betas, log_decay)
    return finish(carried, base, exchange_plain(pairs), out_gain)


def solution(mesh):
    both = ("outer", "inner")
    placed = (P(both, None), P(None, both, None), P(None, both, None), P(None, None, both), P(None, both), P())
    return jax.shard_map(
        functools.partial(per_device, mesh.shape["inner"], mesh.shape["outer"]),
        mesh=mesh,
        in_specs=placed,
        out_specs=P(both, None),
        check_vma=False,
    )
```

profile of v0, /device:TPU:5, one launch (start us, length us, event | category | flops | bytes accessed | tf_op | source)
XLA Modules:
  0.0 55.1 jit_solution(11688194237282795003)
XLA Ops:
  0.0 0.8 %reshape.15 = f32[8,4,1,64]{3,1,0,2:T(4,128)S(1)} reshape(f32[8,256]{1,0:T(8,128)} %param.10) | data formatting | bytes 16384 | tf_op jit(solution)/shard_map/reshape | solution.py:152
  0.8 0.0 copy-start
  0.8 0.1 reshape.16
  0.9 0.6 %copy-done = f32[2,8,256]{2,1,0:T(8,128)S(1)} copy-done((f32[2,8,256]{2,1,0:T(8,128)S(1)}, f32[2,8,256]{2,1,0:T(8,128)}, u32[]{:S(2)}) %copy-start) | copy-done | bytes 16408
  1.5 0.1 reshape.17
  1.7 0.1 reshape.18
  1.7 0.6 %pad_maximum_fusion.1.s_ref = f32[8,8,128]{2,1,0:T(8,128)} fusion(f32[8,4,128]{2,1,0:T(4,128)S(1)} %reshape.18, f32[8,4,128]{2,1,0:T(4,128)S(1)} %reshape.16), kind=kLoop, calls=%fused_computation.1 | loop fusion | flops 8192 | bytes 65536 | tf_op jit(solution)/shard_map/concatenate | solution.py:154
  2.4 50.9 %whole.1 = bf16[256,1024]{1,0:T(8,128)(2,1)} custom-call(bf16[256,1024]{1,0:T(8,128)(2,1)} %q_ref.1, bf16[2,256,1024]{2,1,0:T(8,128)(2,1)} %k_ref.1, bf16[2,256,1024]{2,1,0:T(8,128)(2,1)} %v_ref.1, f32[8,8,128]{2,1,0:T(8,128)} %pad_maximum_fusion.1.s_ref, f32[1,128]{1,0:T(1,128)} %bitcast.7), custom_call_target="tpu_custom_call" | custom-call | tf_op jit(solution)/shard_map/whole/pallas_call | solution.py:380
  53.2 1.9 %copy.13 = bf16[256,1024]{1,0:T(8,128)(2,1)} copy(bf16[256,1024]{1,0:T(8,128)(2,1)} %whole.1) | data formatting | bytes 1048576
  (2 shorter events, 0.1 us)
Async XLA Ops:
  0.8 0.7 %copy-start = (f32[2,8,256]{2,1,0:T(8,128)S(1)}, f32[2,8,256]{2,1,0:T(8,128)}, u32[]{:S(2)}) copy-start(f32[2,8,256]{2,1,0:T(8,128)} %param.9) | copy-start | bytes 49156
where the time goes:
time: 55.4 us; the launch traced here: 55.1 us
  Pallas kernels  50.9 us (92%)
  local copies, waits for them, and re-layouts  3.56 us (6%)
  other arithmetic  0.66 us (1%)
    pallas_call x1, Pallas kernels, whole(): pl.pallas_call(functools.partial(whole_kernel, inner, outer), in_specs=[v...  50.9 us
    unnamed x3, local copies, waits for them, and re-layouts  2.49 us

commit v1 on v0

--- a/solution.py
+++ b/solution.py
@@ -40,100 +40,191 @@
     return dot(a2, jnp.concatenate([bh, bh], 0)) + dot(a2[:, :128], bl)
 
 
-def mul_left(a, b):
-    return dot(wide(a), jnp.concatenate([b, b], 0))
-
-
 def add_right(x, y):
     return jnp.concatenate([x[:, :128], x[:, 128:] + y], 1)
 
 
-def masks():
+def apply3(a, b):
+    ah, al = split(a)
+    bh, bl = split(b)
+    return dot(jnp.concatenate([ah, al], 1), jnp.concatenate([bh, bh], 0)) + dot(ah, bl)
+
+
+def gathered_rows(decay, beta0, beta1):
+    lane = lax.broadcasted_iota(jnp.int32, decay.shape[:1] + (128,), 1)
+    group = lane >> 4
+    out = []
+    for half in range(decay.shape[1] // 128):
+        at = slice(128 * half, 128 * half + 128)
+        c, b0, b1 = decay[:, at], beta0[:, at], beta1[:, at]
+        width = 1
+        while width < BLOCK_LEN:
+            c = c + jnp.where((lane & (BLOCK_LEN - 1)) >= width, pltpu.roll(c, width, 1), 0.0)
+            width *= 2
+        for first in (0, BLOCK_LEN):
+
+            def moved(x, step):
+                shift = (16 * step - first) % 128
+                return pltpu.roll(x, shift, 1) if shift else x
+
+            c_row = moved(c, 0)
+            beta_row = moved(b0, 0)
+            for g in range(1, 8):
+                step = g // 2 + g % 2
+                c_row = jnp.where(group == g, moved(c, step), c_row)
+                beta_row = jnp.where(group == g, moved(b1 if g % 2 else b0, step), beta_row)
+            out.append((c_row, beta_row))
+    return out
+
+
+def mixed_rows(x0, x1):
+    parts = []
+    for at in range(0, BLOCK_LEN, 16):
+        parts += [x0[at : at + 16], x1[at : at + 16]]
+    return jnp.concatenate(parts, 0)
+
+
+def rank_of(x):
+    return 2 * (16 * (x >> 5) + (x & 15)) + ((x >> 4) & 1)
+
+
+def product3(ah, al, bh, bl):
+    rows = ah.shape[0]
+    o = dot(jnp.concatenate([ah, al], 0), jnp.concatenate([bh, bl], 1))
+    return o[:rows, :128] + (o[:rows, 128:] + (o[rows:, :128] + o[rows:, 128:]))
+
+
+def head_maps(blocks, heads_in, load, emit, middle=None):
     span = BLOCK_LEN
     size = 2 * span
     row = lax.broadcasted_iota(jnp.int32, (size, size), 0)
     col = lax.broadcasted_iota(jnp.int32, (size, size), 1)
-    row_t, col_t = row & (span - 1), col & (span - 1)
-    row_rank = 2 * row_t + (row >= span).astype(jnp.int32)
-    col_rank = 2 * col_t + (col >= span).astype(jnp.int32)
-    differ = row_rank ^ col_rank
     eye = row == col
     eye_f = eye.astype(F32)
-    lower = row_rank > col_rank
-    c_mask = (col_t <= row_t) & (col < span)
-    r_mask = (row_t <= col_t) & (row < span)
+    lower = (rank_of(row) > rank_of(col)).astype(F32)
+    token = rank_of(col) >> 1
+    seen = (token[:span] <= row[:span]).astype(F32)
+    own = (token[:span] == row[:span]) & ((col[:span] & 16) == 0)
+    row_c, col_c = row[:32], col[:32] & 31
+    rank_r, rank_c = rank_of(row_c), rank_of(col_c)
+    differ = rank_r ^ rank_c
+    eye_c = (row_c == col_c).astype(F32)
     levels = []
-    width = 1
-    while width < size:
-        levels.append(
-            (differ >= width) & (differ < 2 * width) & lower
-        )
-        width *= 2
-
-    return row, col_t, row_t, eye, eye_f, lower, c_mask, r_mask, levels
-
-
-def head_maps(blocks, heads_in, load, emit):
-    span = BLOCK_LEN
-    row, col_t, row_t, eye, eye_f, lower, c_mask, r_mask, levels = masks()
+    for width in (1, 2, 4, 8, 16):
+        levels.append(((differ >= width) & (differ < 2 * width) & (rank_r > rank_c)).astype(BF16))
+    part = (col >> 5)[:32]
+    chunk = [part == c for c in range(4)]
+    zero_c = jnp.zeros((32, 128), BF16)
+
+    def spread(x):
+        return jnp.concatenate([jnp.where(chunk[c], x, zero_c) for c in range(4)], 0)
+
+    def diagonal(x):
+        y = jnp.where(chunk[0], x[:32], x[32:64])
+        y = jnp.where(chunk[2], x[64:96], y)
+        return jnp.where(chunk[3], x[96:], y)
+
+    def below(x):
+        return jnp.where(chunk[0], x[32:64], jnp.where(chunk[2], x[96:], zero_c))
+
     work = []
     for i, n in [(i, n) for i in range(heads_in) for n in range(blocks)]:
-        q_b, k_b, v_b, d_row, beta_row = load(i, n)
-        d_col = jnp.sum(jnp.where(eye, d_row, 0.0), 1, keepdims=True)
-        beta_col = jnp.sum(jnp.where(eye, beta_row, 0.0), 1, keepdims=True)
-        c_col = jnp.sum(jnp.where(c_mask, d_row, 0.0), 1, keepdims=True)
-        c_row = jnp.sum(jnp.where(r_mask, d_col, 0.0), 0, keepdims=True)
-        gram = dot_t(k_b, k_b)
-        k_f = k_b.astype(F32)
+        q_b, k_b, v_b, c_row, beta_row = load(i, n)
+        both = dot_t(jnp.concatenate([k_b, q_b], 0), k_b)
+        gram, cross = both[:size], both[size:]
         q_f = q_b.astype(F32)
-        ki_col = lax.rsqrt(jnp.sum(k_f * k_f, 1, keepdims=True) + 1e-06)
         ki_row = lax.rsqrt(jnp.sum(jnp.where(eye, gram, 0.0), 0, keepdims=True) + 1e-06)
         qi_col = lax.rsqrt(jnp.sum(q_f * q_f, 1, keepdims=True) + 1e-06)
-        fall = jnp.exp(jnp.minimum(c_col - c_row, 0.0))
-        low = jnp.where(lower, gram * (beta_col * ki_col) * ki_row * fall, 0.0)
-        reach = dot_t(q_b, k_b) * qi_col * ki_row * fall[:span]
-        reach = jnp.where(col_t[:span] <= row_t[:span], reach, 0.0)
-        query = q_f * (qi_col * jnp.exp(c_col[:span]))
-        work.append((k_b, v_b, beta_row, c_row, c_col, ki_row, ki_col, low, reach, query))
-
-    inverse = [eye_f - jnp.where(levels[0], w[7], 0.0) for w in work]
+        up = jnp.exp(c_row)
+        key_row = beta_row * ki_row * up
+        away_row = ki_row * jnp.exp(-c_row)
+        last = c_row[:, size - 1 :]
+        tail_row = ki_row * jnp.exp(last - c_row)
+        key_col = jnp.sum(jnp.where(eye, key_row, 0.0), 1, keepdims=True)
+        query_col = qi_col * jnp.sum(jnp.where(own, up, 0.0), 1, keepdims=True)
+        low_h, low_l = split(gram * key_col * away_row * lower)
+        reach = cross * query_col * away_row * seen
+        query = q_f * query_col
+        k_t = jnp.transpose(k_b.astype(F32)) * tail_row
+        work.append(dict(k=k_b, v=v_b, beta=beta_row, key=key_row, last=jnp.exp(last), low_h=low_h, low_l=low_l,
+                         left=jnp.concatenate([reach, k_t], 0), query=query))
+
+    for w in work:
+        w["dh"], w["dl"] = diagonal(w["low_h"]), diagonal(w["low_l"])
+        first = (w["dh"] * levels[0]).astype(F32) + (w["dl"] * levels[0]).astype(F32)
+        w["t"] = eye_c - first
     for mask in levels[1:]:
-        part = [mul(jnp.where(mask, w[7], 0.0), t) for w, t in zip(work, inverse)]
-        inverse = [t - mul(t, p) for t, p in zip(inverse, part)]
-
-    states = [None] * heads_in
-    for n in range(blocks):
-        for i in range(heads_in):
-            state = states[i]
-            k_b, v_b, beta_row, c_row, c_col, ki_row, ki_col, low, reach, query = work[i * blocks + n]
-            t = inverse[i * blocks + n] * beta_row
-            written = jnp.concatenate(
-                [mul_left(t * (ki_row * jnp.exp(c_row)), k_b), mul_left(t, v_b)], 1
-            )
-            got = mul(reach, written)
-            reduced, local_out = query - got[:, :128], got[:, 128:]
-            last = c_col[span - 1 : span, :]
-            tail = jnp.exp(last - c_col) * ki_col
-            wh, wl = split(written * tail)
-            k_t = jnp.transpose(k_b.astype(F32)).astype(BF16)
-            made = dot(jnp.concatenate([k_t, k_t], 1), jnp.concatenate([wh, wl], 0))
-            trans = jnp.exp(last) * eye_f - made[:, :128]
-            inject = made[:, 128:]
-            if state is None:
-                emit(i, n, reduced, local_out)
-                states[i] = jnp.concatenate([trans, inject], 1)
-            else:
-                read = mul(reduced, state)
-                emit(i, n, read[:, :128], read[:, 128:] + local_out)
-                states[i] = add_right(mul(trans, state), inject)
+        for w in work:
+            w["th"], w["tl"] = split(w["t"])
+            w["p"] = product3(w["dh"] * mask, w["dl"] * mask, spread(w["th"]), spread(w["tl"]))
+        for w in work:
+            ph, pl_ = split(w["p"])
+            w["t"] = w["t"] - product3(w["th"], w["tl"], spread(ph), spread(pl_))
+    if middle is not None:
+        middle()
+    for w in work:
+        w["th"], w["tl"] = split(w["t"])
+        w["p"] = product3(below(w["low_h"]), below(w["low_l"]), spread(w["th"]), spread(w["tl"]))
+    for w in work:
+        ph, pl_ = split(w["p"])
+        rh, rl = split(pltpu.roll(w["t"], 96, 1))
+        w["p"] = product3(rh, rl, spread(ph), spread(pl_))
+    for w in work:
+        t, p = w["t"], w["p"]
+        w["ta"] = jnp.concatenate(
+            [jnp.where(chunk[0], t, 0.0), jnp.where(chunk[1], t, jnp.where(chunk[0], -p, 0.0))], 0
+        )
+        w["tb"] = jnp.concatenate(
+            [jnp.where(chunk[2], t, 0.0), jnp.where(chunk[3], t, jnp.where(chunk[2], -p, 0.0))], 0
+        )
+        ah, al = split(w["ta"])
+        w["p"] = product3(w["low_h"][span:, :span], w["low_l"][span:, :span], ah, al)
+    zero_s = jnp.zeros((span, size), BF16)
+    for w in work:
+        ph, pl_ = split(w["p"])
+        bh, bl = split(w["tb"])
+        w["tb"] = w["tb"] - product3(
+            bh, bl, jnp.concatenate([zero_s, ph], 0), jnp.concatenate([zero_s, pl_], 0)
+        )
+
+    for w in work:
+        t = jnp.concatenate([w["ta"], w["tb"]], 0)
+        k2 = jnp.concatenate([w["k"], w["k"]], 0)
+        v2 = jnp.concatenate([w["v"], w["v"]], 0)
+        w["written"] = jnp.concatenate([dot(wide(t * w["key"]), k2), dot(wide(t * w["beta"]), v2)], 1)
+    for w in work:
+        got = apply3(w["left"], w["written"])
+        read = jnp.concatenate([w["query"] - got[:span, :128], got[:span, 128:]], 1)
+        trans = w["last"] * eye_f - got[span:, :128]
+        w["rows"] = jnp.concatenate([read, jnp.concatenate([trans, got[span:, 128:]], 1)], 0)
+
+    level = [[work[i * blocks + n]["rows"] for n in range(blocks)] for i in range(heads_in)]
+    level = [[[x[:span], x[span:]] for x in parts] for parts in level]
+    while len(level[0]) > 1:
+        merged = []
+        for parts in level:
+            pairs = []
+            for first, later in zip(parts[::2], parts[1::2]):
+                moved = jnp.concatenate(later, 0)
+                moved = add_right(apply3(moved[:, :128], first[-1]), moved[:, 128:])
+                cut = span * (len(later) - 1)
+                pairs.append(first[:-1] + [moved[span * j : span * (j + 1)] for j in range(len(later) - 1)] + [moved[cut:]])
+            merged.append(pairs)
+        level = merged
+    states = []
+    for i in range(heads_in):
+        parts = level[i][0]
+        for n in range(blocks):
+            emit(i, n, parts[n][:, :128], parts[n][:, 128:])
+        states.append(parts[-1])
     return states
 
 
 def local_kernel(blocks, q_ref, k_ref, v_ref, s_ref, x_ref, c_ref, b_ref):
     def load(i, n):
         at = pl.ds(n * BLOCK_LEN, BLOCK_LEN)
-        k_b = jnp.concatenate([k_ref[0, at, :], k_ref[1, at, :]], 0)
-        v_b = jnp.concatenate([v_ref[0, at, :], v_ref[1, at, :]], 0)
+        k_b = mixed_rows(k_ref[0, at, :], k_ref[1, at, :])
+        v_b = mixed_rows(v_ref[0, at, :], v_ref[1, at, :])
         return q_ref[at, :], k_b, v_b, s_ref[0, n : n + 1, :], s_ref[0, blocks + n : blocks + n + 1, :]
 
     def emit(i, n, carried, base):
@@ -147,12 +238,12 @@
 def small_rows(betas, log_decay):
     heads, length = log_decay.shape
     blocks = length // BLOCK_LEN
-    beta = betas.reshape(2, heads, blocks, BLOCK_LEN).transpose(1, 2, 0, 3)
+    beta = betas.reshape(2, heads, blocks, BLOCK_LEN // 16, 16).transpose(1, 2, 3, 0, 4)
     beta = beta.reshape(heads, blocks, 2 * BLOCK_LEN)
-    decay = log_decay.reshape(heads, blocks, 1, BLOCK_LEN)
-    decay = jnp.concatenate([decay, decay], 2).reshape(heads, blocks, 2 * BLOCK_LEN)
-    small = jnp.concatenate([decay, beta], 1)
-    return small
+    decay = jnp.cumsum(log_decay.reshape(heads, blocks, BLOCK_LEN), -1)
+    decay = decay.reshape(heads, blocks, BLOCK_LEN // 16, 1, 16)
+    decay = jnp.concatenate([decay, decay], 3).reshape(heads, blocks, 2 * BLOCK_LEN)
+    return jnp.concatenate([decay, beta], 1)
 
 
 def local_phase(queries, keys, values, betas, log_decay):
@@ -194,8 +285,8 @@
 
 
 def whole_kernel(
-    inner, outer, q_ref, k_ref, v_ref, s_ref, g_ref, o_ref,
-    away, near, own, even_map, sent, got, groups, mine, ready, came, aside, beside, c_buf, b_buf,
+    inner, outer, q_ref, k_ref, v_ref, beta_ref, decay_ref, g_ref, o_ref,
+    away, near, own, even_map, sent, got, groups, mine, ready, came, aside, beside, c_buf, b_buf, rows,
     send0, recv0, send1, recv1, send2, recv2, send3, recv3, send4, recv4,
 ):
     mesh_id = pl.DeviceIdType.MESH
@@ -214,7 +305,12 @@
     pl.semaphore_signal(barrier, inc=1, device_id=(group, partner), device_id_type=mesh_id)
     for d in range(1, outer):
         pl.semaphore_signal(barrier, inc=1, device_id=((group + d) % outer, me), device_id_type=mesh_id)
-    pl.semaphore_wait(barrier, chips + outer - 1)
+    for n, (c_row, beta_row) in enumerate(gathered_rows(decay_ref[...], beta_ref[0], beta_ref[1])):
+        rows[n] = c_row
+        rows[blocks + n] = beta_row
+
+    def apart(turn):
+        return chips // 2 + (turn + 1) // 2 * (1 - 2 * (turn % 2))
 
     def near_copy(turn):
         return pltpu.make_async_remote_copy(
@@ -235,36 +331,42 @@
         here, there = own[turn], near[turn]
         even = jnp.where(core == 0, here, there)
         odd = jnp.where(core == 0, there, here)
-        even_map[turn] = even
+        even_map[apart(turn)] = even
         return then(even, odd)
 
     def step(turn, carry):
-        far = (chip + turn + 1) % chips * 2
+        far = (chip + apart(turn)) % chips * 2
         heads = [far + core, far + 1 - core]
 
         def load(i, n):
             at = pl.ds(n * BLOCK_LEN, BLOCK_LEN)
             lanes = pl.ds(pl.multiple_of(heads[i] * 128, 128), 128)
-            k_b = jnp.concatenate([k_ref[0, at, lanes], k_ref[1, at, lanes]], 0)
-            v_b = jnp.concatenate([v_ref[0, at, lanes], v_ref[1, at, lanes]], 0)
-            rows = s_ref[heads[i]]
-            return q_ref[at, lanes], k_b, v_b, rows[n : n + 1], rows[blocks + n : blocks + n + 1]
+            k_b = mixed_rows(k_ref[0, at, lanes], k_ref[1, at, lanes])
+            v_b = mixed_rows(v_ref[0, at, lanes], v_ref[1, at, lanes])
+            one = pl.ds(heads[i], 1)
+            return q_ref[at, lanes], k_b, v_b, rows[n, one, :], rows[blocks + n, one, :]
 
         def emit(i, n, carried, base):
             at = pl.ds(n * BLOCK_LEN, BLOCK_LEN)
             c_buf[heads[i], at, :] = carried
             b_buf[heads[i], at, :] = base
 
-        states = head_maps(blocks, 2, load, emit)
+        def middle():
+            @pl.when(turn == 0)
+            def _():
+                pl.semaphore_wait(barrier, chips + outer - 1)
+
+            @pl.when(turn > 0)
+            def _():
+                to = apart(turn - 1)
+                sent[to] = chip_map(turn - 1)
+                map_copy(to).start()
+
+        states = head_maps(blocks, 2, load, emit, middle)
+
         away[turn] = states[1]
         near_copy(turn).start()
         own[turn] = states[0]
-
-        @pl.when(turn > 0)
-        def _():
-            sent[turn] = chip_map(turn - 1)
-            map_copy(turn).start()
-
         return carry
 
     lax.fori_loop(0, chips, step, 0)
@@ -295,11 +397,24 @@
             device_id=((group + d) % outer, me), device_id_type=mesh_id,
         )
 
+    def first_copy(d):
+        half = (slice(None), pl.ds(128, 128))
+        return pltpu.make_async_remote_copy(
+            src_ref=mine.at[half], dst_ref=groups.at[(d,) + half],
+            send_sem=send2.at[d], recv_sem=recv2.at[d],
+            device_id=((group + d) % outer, me), device_id_type=mesh_id,
+        )
+
     for d in range(1, outer):
 
-        @pl.when(group + d < outer)
+        @pl.when((group + d < outer) & (group > 0))
         def _():
             group_copy(d).start()
+
+    @pl.when(group == 0)
+    def _():
+        for d in range(1, outer):
+            first_copy(d).start()
 
     before = {}
     for i in range(1, chips):
@@ -312,16 +427,25 @@
 
     for d in range(1, outer):
 
-        @pl.when(group + d < outer)
+        @pl.when((group + d < outer) & (group > 0))
         def _():
             group_copy(d).wait_send()
 
-        @pl.when(group - d >= 0)
+        @pl.when(group - d > 0)
         def _():
             group_copy(d).wait_recv()
 
-    start = jnp.zeros((128, 128), F32)
-    for g in range(outer - 1):
+        @pl.when(group == d)
+        def _():
+            first_copy(d).wait_recv()
+
+    @pl.when(group == 0)
+    def _():
+        for d in range(1, outer):
+            first_copy(d).wait_send()
+
+    start = jnp.where(group > 0, groups[group][:, 128:], 0.0)
+    for g in range(1, outer - 1):
         pair = groups[(group - g + outer) % outer]
         moved = mul(pair[:, :128], start) + pair[:, 128:]
         start = jnp.where(g < group, moved, start)
@@ -360,7 +484,7 @@
             enter = came[d]
         else:
             enter = ready[chip]
-        pair = even_map[chips - 1 - d]
+        pair = even_map[(chips - d) % chips]
         after = mul(pair[:, :128], enter) + pair[:, 128:]
         aside[d] = jnp.where(core == 0, after, enter)
         side_copy(d).start()
@@ -379,7 +503,7 @@
     dma = pltpu.SemaphoreType.DMA
     return pl.pallas_call(
         functools.partial(whole_kernel, inner, outer),
-        in_specs=[vmem] * 5,
+        in_specs=[vmem] * 6,
         out_specs=vmem,
         out_shape=jax.ShapeDtypeStruct((length, width), BF16),
         scratch_shapes=[
@@ -388,13 +512,14 @@
             pltpu.VMEM((128, 256), F32),
             *[pltpu.VMEM((inner // 2, 128, 128), F32)] * 4,
             *[pltpu.VMEM((inner, length, 128), F32)] * 2,
+            pltpu.VMEM((2 * (length // BLOCK_LEN), inner, 128), F32),
             *[dma((inner // 2,))] * 4,
             *[dma((outer,))] * 2,
             *[dma((inner // 2,))] * 4,
         ],
         compiler_params=pltpu.CompilerParams(collective_id=0, has_side_effects=True),
         name="whole",
-    )(queries, keys, values, small_rows(betas, log_decay), out_gain.reshape(1, 128))
+    )(queries, keys, values, betas, log_decay, out_gain.reshape(1, 128))
 
 
 HIGHEST = lax.Precision.HIGHEST

time: 55.4 us -> 41.5 us (0.75)
  the two profiles are of different devices: /device:TPU:5 before, /device:TPU:7 now
where the time goes in v1:
time: 41.5 us; the launch traced here: 41.3 us
  Pallas kernels  39.5 us (95%)
  local copies, waits for them, and re-layouts  1.87 us (5%)
    pallas_call x1, Pallas kernels, whole(): pl.pallas_call(functools.partial(whole_kernel, inner, outer), in_specs=[v...  39.5 us
    unnamed x1, local copies, waits for them, and re-layouts  1.87 us

profile of v1, /device:TPU:7, one launch (start us, length us, event | category | flops | bytes accessed | tf_op | source)
XLA Modules:
  0.0 41.3 jit_solution(4072736881927420128)
XLA Ops:
  0.0 39.5 %whole.1 = bf16[256,1024]{1,0:T(8,128)(2,1)} custom-call(bf16[256,1024]{1,0:T(8,128)(2,1)} %q_ref.1, bf16[2,256,1024]{2,1,0:T(8,128)(2,1)} %k_ref.1, bf16[2,256,1024]{2,1,0:T(8,128)(2,1)} %v_ref.1, f32[2,8,256]{2,1,0:T(8,128)} %beta_ref.1, f32[8,256]{1,0:T(8,128)} %decay_ref.1, f32[1,128]{1,0:T(1,128)} %bitcast.1), custom_call_target="tpu_custom_call" | custom-call | tf_op jit(solution)/shard_map/whole/pallas_call | solution.py:504
  39.5 1.9 %copy.8 = bf16[256,1024]{1,0:T(8,128)(2,1)} copy(bf16[256,1024]{1,0:T(8,128)(2,1)} %whole.1) | data formatting | bytes 1048576
